TPU v7x, 32 devices: a whole 2x2x4 slice. The times are simulated.
32 devices in a mesh: fsdp: 8 (over z, x), ctx: 4 (over y, core).
Axes of the slice: x: 2, y: 2, z: 4, core: 2. Of those that a mesh axis runs over, the one named last changes fastest.
Arguments:
- block_input: bfloat16 [4096, 1024], P(('fsdp', 'ctx')), may hold values from -6 to 6
- attn_gain: bfloat16 [1024], P('fsdp'), may hold values from 0.25 to 1.75
- query_proj: bfloat16 [1024, 1024], P('fsdp'), may hold values from -0.1875 to 0.1875
- key_proj: bfloat16 [1024, 512], P('fsdp'), may hold values from -0.1875 to 0.1875
- value_proj: bfloat16 [1024, 512], P('fsdp'), may hold values from -0.1875 to 0.1875
- qk_gain: bfloat16 [128], P('fsdp'), may hold values from 0.099609375 to 1.8984375
- out_proj: bfloat16 [1024, 1024], P('fsdp'), may hold values from -0.75 to 0.75
- ffn_gain: bfloat16 [1024], P('fsdp'), may hold values from 0.25 to 1.75
- gate_proj: bfloat16 [4608, 1024], P('fsdp'), may hold values from -0.1875 to 0.1875
- up_proj: bfloat16 [4608, 1024], P('fsdp'), may hold values from -0.1875 to 0.1875
- down_proj: bfloat16 [4608, 1024], P('fsdp'), may hold values from -0.09375 to 0.09375
- seg_lengths: int32 [8, 4], P('fsdp'), may hold values from 1 to 256, 512 in all within a row
- out_cotangent: bfloat16 [4096, 1024], P(('fsdp', 'ctx')), may hold values from -6 to 6
Outputs:
- block_output: bfloat16 [4096, 1024], P(('fsdp', 'ctx'))
- input_grad: float32 [4096, 1024], P(('fsdp', 'ctx'))
- attn_gain_grad: float32 [1024], P('fsdp')
- query_grad: float32 [1024, 1024], P(('fsdp', 'ctx'))
- key_grad: float32 [1024, 512], P(('fsdp', 'ctx'))
- value_grad: float32 [1024, 512], P(('fsdp', 'ctx'))
- qk_gain_grad: float32 [128], P('fsdp')
- out_proj_grad: float32 [1024, 1024], P(('fsdp', 'ctx'))
- ffn_gain_grad: float32 [1024], P('fsdp')
- gate_grad: float32 [4608, 1024], P(('fsdp', 'ctx'))
- up_grad: float32 [4608, 1024], P(('fsdp', 'ctx'))
- down_grad: float32 [4608, 1024], P(('fsdp', 'ctx'))
Inputs may be any that keep to these rules, and one draw needn't show every extreme that they name: `seg_lengths`: each row holds the lengths of the 4 segments of one group; they sum to 512.
All inputs are finite; a program needn't handle non-finite values.
Results may differ from a plain program's by a relative error of at most 0.017.
Values may be sent and summed in bfloat16 or wider, within the bound.
A program may use at most 256 MiB of HBM per device.

v0:
```python
import jax
import jax.numpy as jnp
from jax import lax
from jax.experimental import pallas as pl
from jax.experimental.pallas import tpu as pltpu
from jax.sharding import PartitionSpec as P

H = 16
KVH = 8
HEAD = 64


epsilon = 1e-05
rope_base = 1000000.0
masked_score = -1e30


def rms_scale(values):
    return lax.rsqrt(jnp.mean(values * values, axis=-1, keepdims=True) + epsilon)


def norm_back(values, inv_rms, gain_vec, upstream):
    scaled_up = upstream * gain_vec
    return inv_rms * scaled_up - values * (inv_rms * inv_rms * inv_rms) * jnp.mean(
        scaled_up * values, axis=-1, keepdims=True
    )


def segment_positions(lengths, token_count):
    seg_ends = jnp.cumsum(lengths)
    seg_starts = seg_ends - lengths
    token_index = jnp.arange(token_count, dtype=jnp.int32)
    segment = jnp.sum((token_index[:, None] >= seg_ends[None, :]).astype(jnp.int32), axis=1)
    seg_begin = jnp.max(
        jnp.where(token_index[:, None] >= seg_starts[None, :], seg_starts[None, :], 0), axis=1
    )
    return (segment, token_index - seg_begin)


def rope_tables(positions, head_width):
    half_width = head_width // 2
    frequency = rope_base ** (-(jnp.arange(half_width, dtype=jnp.float32) * 2.0 / head_width))
    angle_all = positions.astype(jnp.float32)[:, None] * frequency[None, :]
    return (jnp.cos(angle_all), jnp.sin(angle_all))


def rotate(values, cos_tab, sine_tab):
    half_width = values.shape[-1] // 2
    front_half = values[..., :half_width]
    back_half = values[..., half_width:]
    cos_b = cos_tab[:, None, :]
    sin_b = sine_tab[:, None, :]
    return jnp.concatenate(
        [front_half * cos_b - back_half * sin_b, back_half * cos_b + front_half * sin_b], axis=-1
    )


def unrotate(upstream, cos_tab, sine_tab):
    half_width = upstream.shape[-1] // 2
    front_half = upstream[..., :half_width]
    back_half = upstream[..., half_width:]
    cos_b = cos_tab[:, None, :]
    sin_b = sine_tab[:, None, :]
    return jnp.concatenate(
        [front_half * cos_b + back_half * sin_b, back_half * cos_b - front_half * sin_b], axis=-1
    )


def dot_nn(left_mat, right_mat):
    return jnp.dot(left_mat, right_mat, preferred_element_type=jnp.float32)


def dot_nt(left_mat, right_mat):
    return lax.dot_general(
        left_mat, right_mat, (((1,), (1,)), ((), ())), preferred_element_type=jnp.float32
    )


def dot_tn(left_mat, right_mat):
    return lax.dot_general(
        left_mat, right_mat, (((0,), (0,)), ((), ())), preferred_element_type=jnp.float32
    )


MESH = pl.DeviceIdType.MESH
BF = jnp.bfloat16
F32 = jnp.float32


def factor(name):
    count = lax.axis_size(name)
    if name == "ctx":
        direct = 2
    else:
        direct = 1
        while direct * direct * 4 <= count:
            direct *= 2
    return count // direct, direct


class Place:
    def __init__(self, name):
        self.name = name
        self.L, self.D = factor(name)
        index = lax.axis_index(name)
        self.l = index // self.D
        self.d = index % self.D

    def dev(self, l, d):
        return {self.name: l * self.D + d}

    def off(self, dd):
        return lax.rem(self.d + dd, self.D)


def remote(src, dst, ssem, rsem, dev):
    return pltpu.make_async_remote_copy(
        src_ref=src, dst_ref=dst, send_sem=ssem, recv_sem=rsem, device_id=dev, device_id_type=MESH
    )


def add_rows(dst, parts, lead):
    rows = dst.shape[-2]
    step = 16 if rows % 16 == 0 else rows

    def one(pick):
        def body(i, carry):
            at = pl.ds(pl.multiple_of(i * step, step), step) if step != rows else slice(None)
            if dst.dtype == BF and len(parts) == 2:
                pick(dst)[at, :] = pick(parts[0])[at, :] + pick(parts[1])[at, :]
                return carry
            total = pick(parts[0])[at, :].astype(F32)
            for part in parts[1:]:
                total = total + pick(part)[at, :].astype(F32)
            pick(dst)[at, :] = total.astype(dst.dtype)
            return carry

        if step == rows:
            body(0, 0)
        else:
            lax.fori_loop(0, rows // step, body, 0)

    if lead is None:
        one(lambda ref: ref)
    else:
        for j in range(lead):
            one(lambda ref, j=j: ref.at[j])


def line_neighbors(p, act):
    @pl.when(p.l > 0)
    def _():
        act(-1)

    @pl.when(p.l < p.L - 1)
    def _():
        act(1)


def pieces(rows, most):
    for count in range(most, 1, -1):
        if rows % (16 * count) == 0:
            return count
    return 1


def cut(first, rows, size):
    res = []
    while rows > 0:
        take = min(size, rows)
        res.append((first, take, "line"))
        first, rows = first + take, rows - take
    return res


class Gather:
    def __init__(self, name, shape, dtype, split):
        self.name, self.shape, self.dtype = name, shape, dtype
        self.L, self.D = factor(name)
        rows = shape[0]
        self.parts = []
        if split == "both":
            units = rows // 16
            lead = max(1, units // 8)
            self.parts = cut(0, rows - lead * 16, 32) + [(rows - lead * 16, lead * 16, "dir")]
        elif pieces(rows, 4) > 1:
            count = pieces(rows, 4)
            size = rows // count
            self.parts = [(i * size, size, split) for i in range(count)]
        else:
            self.parts = [(0, rows, split)]
        self.outs = [jax.ShapeDtypeStruct((self.L, self.D) + shape, dtype)]
        self.scratch = []
        dma = pltpu.SemaphoreType.DMA
        L, D = self.L, self.D
        for _, _, kind in self.parts:
            if kind == "line":
                self.scratch += [dma((2, L)), dma((L,)), dma((D, L)), dma((D, L))]
            else:
                self.scratch += [dma((D,)), dma((D,)), dma((D, 2, L)), dma((D, L))]

    def gens(self, p, ins, outs, scr):
        src, out = ins[0], outs[0]
        res = []
        for i, (r0, r, kind) in enumerate(self.parts):
            f = self.line_first if kind == "line" else self.dir_first
            res.append((0, f(p, src, out, r0, r, scr[4 * i : 4 * i + 4], i == 0)))
        return res

    def line_first(self, p, src, out, r0, r, sems, keep):
        ls, lr, ds, dr = sems
        L, D, l, d = p.L, p.D, p.l, p.d
        own = src.at[pl.ds(r0, r), :]

        def V(q, dd):
            return out.at[q, dd, pl.ds(r0, r), :]

        def line(q, dirn, view):
            return remote(view, V(q, d), ls.at[(dirn + 1) // 2, q], lr.at[q], p.dev(l + dirn, d))

        def direct(q, view, k):
            return remote(view, V(q, d), ds.at[k - 1, q], dr.at[k - 1, q], p.dev(l, p.off(k)))

        line_neighbors(p, lambda dirn: line(l, dirn, own).start())
        for k in range(1, D):
            direct(l, own, k).start()
        if keep:
            out[l, d] = src[...]
        yield
        for k in range(1, L):
            for sgn in (-1, 1):
                q = l + sgn * k

                @pl.when((q >= 0) & (q < L))
                def _(q=q, sgn=sgn):
                    line(q, -sgn, V(q, d)).wait_recv()
                    for m in range(1, D):
                        direct(q, V(q, d), m).start()

                    @pl.when((l - sgn >= 0) & (l - sgn < L))
                    def _():
                        line(q, -sgn, V(q, d)).start()

            yield
        for q in range(L):
            for k in range(1, D):
                w = V(q, p.off(D - k))
                remote(w, w, ds.at[k - 1, q], dr.at[k - 1, q], p.dev(l, p.off(k))).wait_recv()
        yield "drain"
        for q in range(L):
            for k in range(1, D):
                direct(q, V(q, d), k).wait_send()
        for k in range(0, L):
            for sgn in (-1, 1):
                if k == 0:
                    q = l

                    @pl.when((l - sgn >= 0) & (l - sgn < L))
                    def _(sgn=sgn):
                        line(l, -sgn, own).wait_send()
                else:
                    q = l + sgn * k

                    @pl.when((q >= 0) & (q < L) & (l - sgn >= 0) & (l - sgn < L))
                    def _(q=q, sgn=sgn):
                        line(q, -sgn, V(q, d)).wait_send()

    def dir_first(self, p, src, out, r0, r, sems, keep):
        ds, dr, ls, lr = sems
        L, D, l, d = p.L, p.D, p.l, p.d
        own = src.at[pl.ds(r0, r), :]

        def V(q, dd):
            return out.at[q, dd, pl.ds(r0, r), :]

        def line(j, q, dirn, view):
            return remote(
                view,
                V(q, p.off(D - j)),
                ls.at[j, (dirn + 1) // 2, q],
                lr.at[j, q],
                p.dev(l + dirn, d),
            )

        def direct(k):
            return remote(own, V(l, d), ds.at[k - 1], dr.at[k - 1], p.dev(l, p.off(k)))

        for k in range(1, D):
            direct(k).start()
        line_neighbors(p, lambda dirn: line(0, l, dirn, own).start())
        if keep:
            out[l, d] = src[...]
        yield
        for j in range(1, D):
            w = V(l, p.off(D - j))
            remote(w, w, ds.at[j - 1], dr.at[j - 1], p.dev(l, p.off(j))).wait_recv()
            line_neighbors(p, lambda dirn: line(j, l, dirn, w).start())
        yield
        for k in range(1, L):
            for j in range(D):
                for sgn in (-1, 1):
                    q = l + sgn * k

                    @pl.when((q >= 0) & (q < L))
                    def _(q=q, sgn=sgn, j=j):
                        w = V(q, p.off(D - j))
                        line(j, q, -sgn, w).wait_recv()

                        @pl.when((l - sgn >= 0) & (l - sgn < L))
                        def _():
                            line(j, q, -sgn, w).start()

            yield "drain" if k == L - 1 else None
        for k in range(1, D):
            direct(k).wait_send()
        for k in range(0, L):
            for j in range(D):
                for sgn in (-1, 1):
                    q = l + sgn * k if k else l

                    @pl.when((q >= 0) & (q < L) & (l - sgn >= 0) & (l - sgn < L))
                    def _(q=q, sgn=sgn, j=j):
                        line(j, q, -sgn, own if (k == 0 and j == 0) else V(q, p.off(D - j))).wait_send()


class Spread:
    def __init__(self, shape, dtype, chunks):
        self.shape, self.dtype, self.chunks = shape, dtype, chunks
        self.L, self.D = factor("fsdp")
        if lax.axis_size("ctx") != self.L:
            raise ValueError("unsupported mesh")
        self.name = "fsdp"
        self.outs = [jax.ShapeDtypeStruct((self.D,) + shape, dtype)]
        dma = pltpu.SemaphoreType.DMA
        self.scratch = [dma((chunks, 2)), dma((chunks,)), dma((chunks, self.D)), dma((chunks, self.D))]

    def gens(self, p, ins, outs, scr):
        rows = self.shape[0] // self.chunks
        return [(i, self.one(p, ins[0], outs[0], i, rows, scr)) for i in range(self.chunks)]

    def one(self, p, src, out, i, rows, scr):
        ls, lr, ds, dr = scr
        l, d, D = p.l, p.d, p.D
        c = lax.axis_index("ctx")
        own = src.at[pl.ds(i * rows, rows), :]
        at_home = l == c

        def V(dd):
            return out.at[dd, pl.ds(i * rows, rows), :]

        def line(dirn, view):
            return remote(view, V(d), ls.at[i, (dirn + 1) // 2], lr.at[i], p.dev(l + dirn, d))

        def direct(k, view):
            return remote(view, V(d), ds.at[i, k - 1], dr.at[i, k - 1], p.dev(l, p.off(k)))

        @pl.when(at_home)
        def _():
            line_neighbors(p, lambda dirn: line(dirn, own).start())
            for k in range(1, D):
                direct(k, own).start()
            if i == 0:
                out[d] = src[...]

        yield

        @pl.when(l > c)
        def _():
            line(1, V(d)).wait_recv()

            @pl.when(l < p.L - 1)
            def _():
                line(1, V(d)).start()

            for k in range(1, D):
                direct(k, V(d)).start()

        @pl.when(l < c)
        def _():
            line(-1, V(d)).wait_recv()

            @pl.when(l > 0)
            def _():
                line(-1, V(d)).start()

            for k in range(1, D):
                direct(k, V(d)).start()

        yield
        for k in range(1, D):
            w = V(p.off(D - k))
            remote(w, w, ds.at[i, k - 1], dr.at[i, k - 1], p.dev(l, p.off(k))).wait_recv()
        yield "drain"
        for k in range(1, D):
            direct(k, V(d)).wait_send()

        @pl.when((l <= c) & (l > 0))
        def _():
            line(-1, V(d)).wait_send()

        @pl.when((l >= c) & (l < p.L - 1))
        def _():
            line(1, V(d)).wait_send()


class Reduce:
    def __init__(self, name, shape, dtype, most=1, lines=0, first=0, result=F32):
        self.name, self.shape, self.dtype, self.first = name, shape, dtype, first
        self.L, self.D = factor(name)
        L, D = self.L, self.D
        self.outs = [jax.ShapeDtypeStruct(shape, result)]
        dma = pltpu.SemaphoreType.DMA
        self.count = pieces(shape[0], most if L * D <= 8 else min(most, 4))
        unit = (shape[0] // self.count,) + shape[1:]
        self.scratch = []
        self.kinds = ["dir"] * (self.count - lines) + ["line"] * min(lines, self.count)
        for kind in self.kinds:
            if kind == "line":
                self.scratch += [
                    pltpu.VMEM((L, D) + unit, dtype),
                    pltpu.VMEM((L, D) + unit, dtype),
                    pltpu.VMEM((D,) + unit, dtype),
                    pltpu.VMEM((max(D - 1, 1),) + unit, dtype),
                    dma((2, L)),
                    dma((2, L)),
                    dma((D,)),
                    dma((D,)),
                ]
            else:
                self.scratch += [
                    pltpu.VMEM((L,) + unit, dtype),
                    pltpu.VMEM((L,) + unit, dtype),
                    pltpu.VMEM((L,) + unit, dtype),
                    pltpu.VMEM((max(D - 1, 1), L) + unit, dtype),
                    dma((2, L)),
                    dma((2, L)),
                    dma((D, L)),
                    dma((D, L)),
                ]

    def gens(self, p, ins, outs, scr):
        size = self.shape[0] // self.count
        res = []
        for i, kind in enumerate(self.kinds):
            at = pl.ds(i * size, size)
            f = self.line_first if kind == "line" else self.dir_first
            start = 0 if kind == "line" else self.first + i
            res.append((start, f(p, ins[0], outs[0].at[at, :], at, scr[8 * i : 8 * i + 8])))
        return res

    def line_sum(self, p, own, from_left, from_right, ls, lr, lead, prep):
        L, l = p.L, p.l

        def right(q, view):
            return remote(view, from_left.at[q], ls.at[1, q], lr.at[1, q], p.dev(l + 1, p.d))

        def left(q, view):
            return remote(view, from_right.at[q], ls.at[0, q], lr.at[0, q], p.dev(l - 1, p.d))

        for t in range(L):
            qr, ql = L - 1 - t, t
            prep(qr)
            if qr > 0:

                @pl.when(l == 0)
                def _():
                    right(qr, own(qr)).start()

            prep(ql)
            if ql < L - 1:

                @pl.when(l == L - 1)
                def _():
                    left(ql, own(ql)).start()

        yield "late" if L <= 2 else None
        for k in range(1, L - 1):

            @pl.when(l == k)
            def _():
                for q in range(L - 1, k, -1):
                    right(q, from_left.at[q]).wait_recv()
                    add_rows(from_left.at[q], [from_left.at[q], own(q)], lead)
                    right(q, from_left.at[q]).start()

            @pl.when(l == L - 1 - k)
            def _():
                for q in range(L - 1 - k):
                    left(q, from_right.at[q]).wait_recv()
                    add_rows(from_right.at[q], [from_right.at[q], own(q)], lead)
                    left(q, from_right.at[q]).start()

            yield

    def line_total(self, p, own, from_left, from_right, ls, lr, dst, lead):
        l, L = p.l, p.L

        def arrive(way):
            v = (from_left if way == 1 else from_right).at[l]
            remote(v, v, ls.at[way, l], lr.at[way, l], p.dev(l + 1 - 2 * way, p.d)).wait_recv()

        @pl.when(l == 0)
        def _():
            arrive(0)
            add_rows(dst, [own(l), from_right.at[l]], lead)

        @pl.when(l == L - 1)
        def _():
            arrive(1)
            add_rows(dst, [own(l), from_left.at[l]], lead)

        if L > 2:

            @pl.when((l > 0) & (l < L - 1))
            def _():
                arrive(0)
                arrive(1)
                add_rows(dst, [own(l), from_left.at[l], from_right.at[l]], lead)

    def line_drain(self, p, from_left, from_right, ls, lr):
        L, l = p.L, p.l
        for q in range(L):
            if q > 0:

                @pl.when(l < q)
                def _():
                    v = from_left.at[q]
                    remote(v, v, ls.at[1, q], lr.at[1, q], p.dev(l + 1, p.d)).wait_send()

            if q < L - 1:

                @pl.when(l > q)
                def _():
                    v = from_right.at[q]
                    remote(v, v, ls.at[0, q], lr.at[0, q], p.dev(l - 1, p.d)).wait_send()

    def line_first(self, p, src, out, at, scr):
        from_left, from_right, acc, box, ls, lr, ds, dr = scr
        D, l, d = p.D, p.l, p.d

        def own(q):
            return src.at[q, :, at, :]

        yield from self.line_sum(p, own, from_left, from_right, ls, lr, D, lambda q: None)
        self.line_total(p, own, from_left, from_right, ls, lr, acc, D)

        def direct(k):
            return remote(
                acc.at[p.off(k)], box.at[k - 1], ds.at[k - 1], dr.at[k - 1], p.dev(l, p.off(k))
            )

        for k in range(1, D):
            direct(k).start()
        yield "late" if self.L > 2 else None
        for k in range(1, D):
            direct(k).wait_recv()
        add_rows(out, [acc.at[d]] + [box.at[k - 1] for k in range(1, D)], None)
        yield "drain"
        for k in range(1, D):
            direct(k).wait_send()
        self.line_drain(p, from_left, from_right, ls, lr)

    def dir_first(self, p, src, out, at, scr):
        from_left, from_right, acc, box, ls, lr, ds, dr = scr
        L, D, l, d = p.L, p.D, p.l, p.d

        def direct(k, q):
            return remote(
                src.at[q, p.off(k), at, :],
                box.at[k - 1, q],
                ds.at[k - 1, q],
                dr.at[k - 1, q],
                p.dev(l, p.off(k)),
            )

        order = []
        for t in range(L):
            for q in (L - 1 - t, t):
                if q not in order:
                    order.append(q)
        for q in order:
            for k in range(1, D):
                direct(k, q).start()
        yield
        ready = set()

        def prep(q):
            if q in ready:
                return
            ready.add(q)
            for k in range(1, D):
                direct(k, q).wait_recv()
            add_rows(
                acc.at[q], [src.at[q, d, at, :]] + [box.at[k - 1, q] for k in range(1, D)], None
            )

        def own(q):
            return acc.at[q]

        yield from self.line_sum(p, own, from_left, from_right, ls, lr, None, prep)
        self.line_total(p, own, from_left, from_right, ls, lr, out, None)
        yield "drain"
        for q in range(L):
            for k in range(1, D):
                direct(k, q).wait_send()
        self.line_drain(p, from_left, from_right, ls, lr)


def greet(places):
    barrier = pltpu.get_barrier_semaphore()
    count = 0
    for p in places:
        for k in range(1, p.D):
            pl.semaphore_signal(
                barrier, inc=1, device_id=p.dev(p.l, p.off(k)), device_id_type=MESH
            )
        count = count + (p.D - 1)
        line_neighbors(
            p,
            lambda dirn: pl.semaphore_signal(
                barrier, inc=1, device_id=p.dev(p.l + dirn, p.d), device_id_type=MESH
            ),
        )
        count = count + jnp.where(p.l > 0, 1, 0) + jnp.where(p.l < p.L - 1, 1, 0)
    pl.semaphore_wait(barrier, count)


def run_all(live):
    live = sorted(live, key=lambda pair: pair[0])
    late, drains, slot = [], [], 0
    while live:
        for start, g in live:
            if start == slot:
                next(g)
        rest = []
        for start, g in live:
            if start >= slot:
                rest.append((start, g))
                continue
            mark = next(g)
            if mark == "drain":
                drains.append(g)
            elif mark == "late":
                late.append(g)
            else:
                rest.append((start, g))
        live, slot = rest, slot + 1
    for g in late + drains:
        for _ in g:
            pass


def communicate(ops, arrays, cid):
    axes = sorted({op.name for op in ops})
    outs = [shape for op in ops for shape in op.outs]
    scratch = [s for op in ops for s in op.scratch]

    def kernel(*refs):
        ins = refs[: len(arrays)]
        out_refs = refs[len(arrays) : len(arrays) + len(outs)]
        scr = refs[len(arrays) + len(outs) :]
        places = {name: Place(name) for name in axes}
        greet([places[name] for name in axes])
        live = []
        o = s = 0
        for i, op in enumerate(ops):
            live += op.gens(
                places[op.name],
                [ins[i]],
                out_refs[o : o + len(op.outs)],
                scr[s : s + len(op.scratch)],
            )
            o += len(op.outs)
            s += len(op.scratch)
        run_all(live)

    vm = pl.BlockSpec(memory_space=pltpu.VMEM)
    return pl.pallas_call(
        kernel,
        out_shape=outs,
        in_specs=[vm] * len(arrays),
        out_specs=[vm] * len(outs),
        scratch_shapes=scratch,
        compiler_params=pltpu.CompilerParams(
            collective_id=cid, has_side_effects=True, vmem_limit_bytes=62 * 1024 * 1024
        ),
    )(*arrays)


def finish(gains, attn_piece, out_piece, qw, kw, cid):
    F, C = lax.axis_size("fsdp"), lax.axis_size("ctx")
    dma = pltpu.SemaphoreType.DMA

    def kernel(
        g, a, w, g_out, q_out, k_out, v_out, o_out,
        gbox, gsum, cbox, a_out, w_out, gs, gr, cs, cr, as_, ar, ws, wr
    ):
        f, c = lax.axis_index("fsdp"), lax.axis_index("ctx")
        goal = c * F + f
        gf, gc = goal // C, goal % C
        here = f * C + c
        sc, sf = here // F, here % F
        away = goal != here
        barrier = pltpu.get_barrier_semaphore()
        fpeer = [lax.rem(f + k, F) for k in range(F)]
        cpeer = [lax.rem(c + k, C) for k in range(C)]
        for k in range(1, F):
            pl.semaphore_signal(barrier, inc=1, device_id=(fpeer[k], c), device_id_type=MESH)
        for k in range(1, C):
            pl.semaphore_signal(barrier, inc=1, device_id=(f, cpeer[k]), device_id_type=MESH)

        @pl.when(away)
        def _():
            pl.semaphore_signal(barrier, inc=1, device_id=(sf, sc), device_id_type=MESH)

        pl.semaphore_wait(barrier, F + C - 2 + jnp.where(away, 1, 0))

        def gcopy(k):
            return remote(g.at[fpeer[k]], gbox.at[k - 1], gs.at[k], gr.at[k], (fpeer[k], c))

        def acopy(k):
            return remote(a.at[cpeer[k]], a_out.at[c], as_.at[k], ar.at[k], (f, cpeer[k]))

        def arecv(k):
            slot = a_out.at[lax.rem(c + C - k, C)]
            return remote(slot, slot, as_.at[k], ar.at[k], (f, cpeer[k]))

        def wcopy():
            return remote(w, w_out, ws.at[0], wr.at[0], (gf, gc))

        def ccopy(k):
            return remote(gsum, cbox.at[k - 1], cs.at[k], cr.at[k], (f, cpeer[k]))

        for k in range(1, F):
            gcopy(k).start()
        for k in range(1, C):
            acopy(k).start()

        @pl.when(away)
        def _():
            wcopy().start()

        @pl.when(jnp.logical_not(away))
        def _():
            w_out[...] = w[...]

        a_out[c] = a[c]
        total = g[f]
        for k in range(1, F):
            gcopy(k).wait_recv()
            total = total + gbox[k - 1]
        gsum[...] = total
        for k in range(1, C):
            ccopy(k).start()
        for k in range(1, C):
            ccopy(k).wait_recv()
            total = total + cbox[k - 1]
        g_out[...] = total
        for k in range(1, C):
            arecv(k).wait_recv()
        for s in range(C):
            q_out[:, s * qw : (s + 1) * qw] = a_out[s, :, :qw].astype(F32)
            k_out[:, s * kw : (s + 1) * kw] = a_out[s, :, qw : qw + kw].astype(F32)
            v_out[:, s * kw : (s + 1) * kw] = a_out[s, :, qw + kw :].astype(F32)
        for k in range(1, F):
            gcopy(k).wait_send()
        for k in range(1, C):
            acopy(k).wait_send()
            ccopy(k).wait_send()

        @pl.when(away)
        def _():
            wcopy().wait()

        o_out[...] = w_out[...].astype(F32)

    rows = attn_piece.shape[1]
    vm = pl.BlockSpec(memory_space=pltpu.VMEM)
    return pl.pallas_call(
        kernel,
        out_shape=[
            jax.ShapeDtypeStruct(gains.shape[1:], F32),
            jax.ShapeDtypeStruct((rows, C * qw), F32),
            jax.ShapeDtypeStruct((rows, C * kw), F32),
            jax.ShapeDtypeStruct((rows, C * kw), F32),
            jax.ShapeDtypeStruct(out_piece.shape, F32),
        ],
        in_specs=[vm] * 3,
        out_specs=[vm] * 5,
        scratch_shapes=[
            pltpu.VMEM((F - 1,) + gains.shape[1:], F32),
            pltpu.VMEM(gains.shape[1:], F32),
            pltpu.VMEM((C - 1,) + gains.shape[1:], F32),
            pltpu.VMEM(attn_piece.shape, attn_piece.dtype),
            pltpu.VMEM(out_piece.shape, out_piece.dtype),
        ]
        + [dma((F,)), dma((F,)), dma((C,)), dma((C,)), dma((C,)), dma((C,)), dma((1,)), dma((1,))],
        compiler_params=pltpu.CompilerParams(collective_id=cid, has_side_effects=True),
    )(gains, attn_piece, out_piece)


def on_device(
    block_input,
    attn_gain,
    query_proj,
    key_proj,
    value_proj,
    qk_gain,
    out_proj,
    ffn_gain,
    gate_proj,
    up_proj,
    down_proj,
    seg_lengths,
    out_cotangent,
):
    T, W = block_input.shape
    C = lax.axis_size("ctx")
    F = lax.axis_size("fsdp")
    L, D = factor("fsdp")
    CL, CD = factor("ctx")
    G = T * C
    hl, kl, share = H // C, KVH // C, H // KVH
    qw, kw = hl * HEAD, kl * HEAD
    rows = query_proj.shape[0]
    scale_att = HEAD ** (-0.5)
    c = lax.axis_index("ctx")

    w_own = jnp.concatenate(
        [
            lax.dynamic_slice_in_dim(query_proj, c * qw, qw, axis=1),
            lax.dynamic_slice_in_dim(key_proj, c * kw, kw, axis=1),
            lax.dynamic_slice_in_dim(value_proj, c * kw, kw, axis=1),
        ],
        axis=1,
    )
    gain_w, pair_w = attn_gain.shape[0], qk_gain.shape[0]
    g_own = jnp.concatenate(
        [
            jnp.pad(vec[None, :], ((0, 0), (0, 128 - vec.shape[0])))
            for vec in (attn_gain, ffn_gain, qk_gain)
        ]
        + [jnp.zeros((13, 128), BF)],
        axis=0,
    )
    w_all, g_all, wo, x_all = communicate(
        [
            Gather("fsdp", w_own.shape, BF, "both"),
            Gather("fsdp", (16, 128), BF, "line"),
            Spread(out_proj.shape, BF, pieces(out_proj.shape[0], 4)),
            Gather("ctx", (T, W), BF, "line"),
        ],
        [w_own, g_own, out_proj, block_input],
        1,
    )
    x_all = x_all.reshape(G, W)
    w_all = w_all.reshape(W, qw + 2 * kw)
    wo = wo.reshape(qw, W)
    g_all = g_all.reshape(F, 16, 128)
    gain_attn = g_all[:, 0, :gain_w].reshape(W).astype(F32)
    gain_ffn = g_all[:, 1, :gain_w].reshape(W).astype(F32)
    gain_pair = g_all[:, 2, :pair_w].reshape(2 * HEAD).astype(F32)
    gain_query, gain_key = gain_pair[:HEAD], gain_pair[HEAD:]

    segment, positions = segment_positions(seg_lengths[0], G)
    cos_tab, sine_tab = rope_tables(positions, HEAD)
    xa = x_all.astype(F32)
    normed = (xa * rms_scale(xa) * gain_attn).astype(BF)
    qkv = dot_nn(normed, w_all)
    queries = qkv[:, :qw].reshape(G, hl, HEAD)
    keys_raw = qkv[:, qw : qw + kw].reshape(G, kl, HEAD)
    v_kv = qkv[:, qw + kw :].astype(BF).reshape(G, kl, HEAD)
    inv_query = rms_scale(queries)
    q_local = rotate(queries * inv_query * gain_query, cos_tab, sine_tab).astype(BF)
    inv_key = rms_scale(keys_raw)
    k_kv = rotate(keys_raw * inv_key * gain_key, cos_tab, sine_tab).astype(BF)
    k_local = jnp.repeat(k_kv, share, axis=1)
    v_local = jnp.repeat(v_kv, share, axis=1)
    token = jnp.arange(G, dtype=jnp.int32)
    allowed = (segment[:, None] == segment[None, :]) & (token[None, :] <= token[:, None])
    scores = (
        jnp.einsum("qhd,khd->hqk", q_local, k_local, preferred_element_type=F32) * scale_att
    )
    scores = jnp.where(allowed[None], scores, masked_score)
    top = jnp.max(scores, axis=2, keepdims=True)
    log_total = top + jnp.log(jnp.sum(jnp.exp(scores - top), axis=2, keepdims=True))
    prob_full = jnp.exp(scores - log_total)
    prob_bf = prob_full.astype(BF)
    o_local = jnp.einsum("hqk,khd->qhd", prob_bf, v_local, preferred_element_type=F32).astype(BF)
    o_flat = o_local.reshape(G, qw)
    part = dot_nn(o_flat, wo).astype(BF).reshape(CL, CD, T, W)
    attn_sum, dy_all = communicate(
        [Reduce("ctx", (T, W), BF, 2), Gather("fsdp", (T, W), BF, "both")],
        [part, out_cotangent],
        2,
    )
    dy_all = dy_all.reshape(F * T, W)

    x_float = block_input.astype(F32)
    inv_one = rms_scale(x_float)
    mixed_res = x_float + attn_sum
    inv_two = rms_scale(mixed_res)
    ffn_in = (mixed_res * inv_two * gain_ffn).astype(BF)
    (ffn_all,) = communicate([Gather("fsdp", (T, W), BF, "both")], [ffn_in], 3)
    ffn_all = ffn_all.reshape(F * T, W)
    gate_pre = dot_nt(ffn_all, gate_proj)
    up_pre = dot_nt(ffn_all, up_proj)
    gate_sig = jax.nn.sigmoid(gate_pre)
    active = gate_pre * gate_sig
    hidden = (active * up_pre).astype(BF)
    d_hidden = dot_nt(dy_all, down_proj)
    d_gate = (d_hidden * up_pre * gate_sig * (1.0 + gate_pre * (1.0 - gate_sig))).astype(BF)
    d_up = (d_hidden * active).astype(BF)
    ffc = gate_proj.shape[0] // C
    grads = [
        dot_tn(a, b).astype(BF).reshape(CL, CD, ffc, W)
        for a, b in ((d_gate, ffn_all), (d_up, ffn_all), (hidden, dy_all))
    ]
    down_part = dot_nn(hidden, down_proj).astype(BF).reshape(L, D, T, W)
    back_part = (
        (dot_nn(d_gate, gate_proj) + dot_nn(d_up, up_proj)).astype(BF).reshape(L, D, T, W)
    )
    gate_grad, up_grad, down_grad, d_ffn_in, ffn_out = communicate(
        [
            Reduce("ctx", (ffc, W), BF),
            Reduce("ctx", (ffc, W), BF),
            Reduce("ctx", (ffc, W), BF),
            Reduce("fsdp", (T, W), BF, 4),
            Reduce("fsdp", (T, W), BF, 4, 0, 4),
        ],
        grads + [back_part, down_part],
        4,
    )
    block_output = (mixed_res + ffn_out).astype(BF)
    grad_gain_ffn = jnp.sum(d_ffn_in * mixed_res * inv_two, axis=0)
    d_mixed = out_cotangent.astype(F32) + norm_back(mixed_res, inv_two, gain_ffn, d_ffn_in)
    (dm_all,) = communicate([Gather("ctx", (T, W), BF, "line")], [d_mixed.astype(BF)], 5)
    dm_all = dm_all.reshape(G, W)
    d_local = dot_nt(dm_all, wo).astype(BF).reshape(G, hl, HEAD)
    row_delta = jnp.sum(d_local.astype(F32) * o_local.astype(F32), axis=2).T[:, :, None]
    d_prob = jnp.einsum("qhd,khd->hqk", d_local, v_local, preferred_element_type=F32)
    d_score = (prob_full * (d_prob - row_delta) * scale_att).astype(BF)
    dq_rot = jnp.einsum("hqk,khd->qhd", d_score, k_local, preferred_element_type=F32).astype(BF)
    dk_sum = jnp.einsum("hqk,qhd->khd", d_score, q_local, preferred_element_type=F32)
    dv_sum = jnp.einsum("hqk,qhd->khd", prob_bf, d_local, preferred_element_type=F32)
    dk_rot = jnp.sum(dk_sum.reshape(G, kl, share, HEAD), axis=2).astype(BF)
    d_values = jnp.sum(dv_sum.reshape(G, kl, share, HEAD), axis=2).astype(BF)
    d_q_norm = unrotate(dq_rot.astype(F32), cos_tab, sine_tab)
    d_k_norm = unrotate(dk_rot.astype(F32), cos_tab, sine_tab)
    grad_gain_q = jnp.sum(d_q_norm * queries * inv_query, axis=(0, 1))
    grad_gain_k = jnp.sum(d_k_norm * keys_raw * inv_key, axis=(0, 1))
    d_queries = norm_back(queries, inv_query, gain_query, d_q_norm).astype(BF).reshape(G, qw)
    d_keys = norm_back(keys_raw, inv_key, gain_key, d_k_norm).astype(BF).reshape(G, kw)
    d_qkv = jnp.concatenate([d_queries, d_keys, d_values.reshape(G, kw)], axis=1)
    dn_part = dot_nt(d_qkv, w_all).astype(BF).reshape(CL, CD, T, W)
    qkv_part = dot_tn(normed, d_qkv).astype(BF).reshape(L, D, rows, qw + 2 * kw)
    wo_part = dot_tn(o_flat, dm_all).astype(BF).reshape(L, D, qw // F, W)
    d_normed, qkv_sum, wo_sum = communicate(
        [
            Reduce("ctx", (T, W), BF),
            Reduce("fsdp", qkv_part.shape[2:], BF, 2, 0, 0, BF),
            Reduce("fsdp", wo_part.shape[2:], BF, 1, 1, 0, BF),
        ],
        [dn_part, qkv_part, wo_part],
        6,
    )
    grad_gain_attn = jnp.sum(d_normed * x_float * inv_one, axis=0)
    input_grad = d_mixed + norm_back(x_float, inv_one, gain_attn, d_normed)
    pair = jnp.concatenate([grad_gain_q, grad_gain_k])
    gains = jnp.concatenate(
        [
            jnp.pad(vec.reshape(F, 1, -1), ((0, 0), (0, 0), (0, 128 - vec.shape[0] // F)))
            for vec in (grad_gain_attn, grad_gain_ffn, pair)
        ]
        + [jnp.zeros((F, 5, 128), F32)],
        axis=1,
    )
    g_sum, query_grad, key_grad, value_grad, out_proj_grad = finish(
        gains, qkv_sum.reshape(C, rows // C, qw + 2 * kw), wo_sum, qw, kw, 7
    )
    return (
        block_output,
        input_grad,
        g_sum[0, :gain_w],
        query_grad,
        key_grad,
        value_grad,
        g_sum[2, :pair_w],
        out_proj_grad,
        g_sum[1, :gain_w],
        gate_grad,
        up_grad,
        down_grad,
    )


def solution(mesh):
    return jax.shard_map(
        on_device,
        mesh=mesh,
        in_specs=(
            P(("fsdp", "ctx"), None),
            P("fsdp"),
            P("fsdp", None),
            P("fsdp", None),
            P("fsdp", None),
            P("fsdp"),
            P("fsdp", None),
            P("fsdp"),
            P("fsdp", None),
            P("fsdp", None),
            P("fsdp", None),
            P("fsdp", None),
            P(("fsdp", "ctx"), None),
        ),
        out_specs=(
            P(("fsdp", "ctx"), None),
            P(("fsdp", "ctx"), None),
            P("fsdp"),
            P(("fsdp", "ctx"), None),
            P(("fsdp", "ctx"), None),
            P(("fsdp", "ctx"), None),
            P("fsdp"),
            P(("fsdp", "ctx"), None),
            P("fsdp"),
            P(("fsdp", "ctx"), None),
            P(("fsdp", "ctx"), None),
            P(("fsdp", "ctx"), None),
        ),
        check_vma=False,
    )
```

profile of v0, /device:TPU:0, one launch (start us, length us, event | category | flops | bytes accessed | tf_op | source)
XLA Modules:
  0.0 295.9 jit_solution(17171382986987615672)
XLA Ops:
  4.5 25.6 %shard_map.220 = (bf16[4,2,128,512]{3,2,1,0:T(8,128)(2,1)}, bf16[4,2,16,128]{3,2,1,0:T(8,128)(2,1)}, bf16[2,128,1024]{2,1,0:T(8,128)(2,1)}, bf16[2,2,128,1024]{3,2,1,0:T(8,128)(2,1)}) custom-call(bf16[128,512]{1,0:T(8,128)(2,1)} %pad_maximum_fusion.10.refs_0_, bf16[16,128]{1,0:T(8,128)(2,1)} %fusion.26.refs_1_, bf16[128,1024]{1,0:T(8,128)(2,1)} %refs_2_.1, ...), custom_call_target="tpu_custom_call" | custom-call | tf_op jit(solution)/shard_map/pallas_call | solution.py:678
  46.5 38.2 %shard_map.221 = (f32[128,1024]{1,0:T(8,128)}, bf16[4,2,128,1024]{3,2,1,0:T(8,128)(2,1)}) custom-call(bf16[2,2,128,1024]{3,2,1,0:T(8,128)(2,1)} %bitcast.166, bf16[128,1024]{1,0:T(8,128)(2,1)} %refs_1_.1), custom_call_target="tpu_custom_call" | custom-call | tf_op jit(solution)/shard_map/pallas_call | solution.py:678
  89.0 26.0 %shard_map.222 = bf16[4,2,128,1024]{3,2,1,0:T(8,128)(2,1)} custom-call(bf16[128,1024]{1,0:T(8,128)(2,1)} %multiply_convert_fusion.5.refs_0_), custom_call_target="tpu_custom_call" | custom-call | tf_op jit(solution)/shard_map/pallas_call | solution.py:678
  114.9 3.5 %fusion.42 = f32[1024,576]{0,1:T(8,128)S(1)} fusion(bf16[1024,1024]{1,0:T(8,128)(2,1)} %bitcast.168, bf16[576,1024]{1,0:T(8,128)(2,1)} %param.21), kind=kOutput, calls=%fused_computation.147 | convolution fusion | flops 1207959552 | bytes 5636096 | tf_op jit(solution)/shard_map/dot_general | solution.py:74
  120.0 2.3 multiply_convert_fusion.1
  122.4 2.5 convolution_convert_fusion.3
  124.9 2.4 convolution_convert_fusion.2
  127.3 2.4 convolution_convert_fusion.1
  129.7 1.9 fusion.43
  131.6 3.3 %add_convert_fusion = bf16[1024,1024]{1,0:T(8,128)(2,1)} fusion(f32[1024,1024]{1,0:T(8,128)S(1)} %fusion.43, bf16[1024,576]{0,1:T(8,128)(2,1)S(1)} %get-tuple-element.60, bf16[576,1024]{1,0:T(8,128)(2,1)S(1)} %copy-done), kind=kOutput, calls=%fused_computation.1 | convolution fusion | flops 1210056704 | bytes 8650752 | tf_op jit(solution)/shard_map/dot_general | solution.py:70
  134.9 3.4 %convolution_convert_fusion = bf16[1024,1024]{1,0:T(8,128)(2,1)} fusion(bf16[1024,576]{0,1:T(8,128)(2,1)S(1)} %get-tuple-element.58, bf16[576,1024]{1,0:T(8,128)(2,1)S(1)} %copy-done.50), kind=kOutput, calls=%fused_computation.17 | convolution fusion | flops 1209008128 | bytes 4456448 | tf_op jit(solution)/shard_map/dot_general | solution.py:70
  138.4 66.1 %shard_map.223 = (f32[144,1024]{1,0:T(8,128)}, f32[144,1024]{1,0:T(8,128)}, f32[144,1024]{1,0:T(8,128)}, f32[128,1024]{1,0:T(8,128)}, f32[128,1024]{1,0:T(8,128)}) custom-call(bf16[2,2,144,1024]{3,2,1,0:T(8,128)(2,1)} %bitcast.174, bf16[2,2,144,1024]{3,2,1,0:T(8,128)(2,1)} %bitcast.175, bf16[2,2,144,1024]{3,2,1,0:T(8,128)(2,1)} %bitcast.176, ...), custom_call_target="tpu_custom_call" | custom-call | tf_op jit(solution)/shard_map/pallas_call | solution.py:678
  204.5 1.8 multiply_reduce_fusion.1
  206.3 2.5 fusion.38
  208.9 10.5 %shard_map.224 = bf16[2,2,128,1024]{3,2,1,0:T(8,128)(2,1)} custom-call(bf16[128,1024]{1,0:T(8,128)(2,1)} %get-tuple-element.54.refs_0_), custom_call_target="tpu_custom_call" | custom-call | tf_op jit(solution)/shard_map/pallas_call | solution.py:678
  219.3 1.9 multiply_reduce_fusion.3
  221.3 4.2 %bitcast_reduce_fusion = bf16[512,2,64]{0,2,1:T(8,128)(2,1)} fusion(bf16[512,4,64]{0,2,1:T(8,128)(2,1)S(1)} %bitcast.213, f32[4,512,512]{1,2,0:T(8,128)} %copy-done.6, f32[4,512]{1,0:T(4,128)S(1)} %copy-done.41, pred[512,512]{0,1:T(8,128)(4,1)S(1)} %copy-done.16), kind=kOutput, calls=%fused_computation.51 | convolution fusion | flops 138477568 | bytes 4857856 | tf_op jit(solution)/shard_map/hqk,qhd->khd/dot_general | solution.py:945
  230.1 2.2 fusion.6
  233.2 3.1 %convolution_convert_fusion.6 = bf16[512,1024]{1,0:T(8,128)(2,1)} fusion(bf16[1024,512]{1,0:T(8,128)(2,1)} %bitcast.210, bf16[512,128]{0,1:T(8,128)(2,1)} %bitcast.215, bf16[512,128]{0,1:T(8,128)(2,1)S(1)} %get-tuple-element.64, bf16[512,256]{0,1:T(8,128)(2,1)S(1)} %get-tuple-element.62), kind=kOutput, calls=%fused_computation.23 | convolution fusion | flops 538968064 | bytes 2621440 | tf_op jit(solution)/shard_map/dot_general | solution.py:74
  236.7 1.8 convolution_convert_fusion.5
  239.7 28.2 %shard_map.225 = (f32[128,1024]{1,0:T(8,128)}, bf16[128,512]{1,0:T(8,128)(2,1)}, bf16[32,1024]{1,0:T(8,128)(2,1)}) custom-call(bf16[2,2,128,1024]{3,2,1,0:T(8,128)(2,1)} %bitcast.180, bf16[4,2,128,512]{3,2,1,0:T(8,128)(2,1)} %bitcast.181, bf16[4,2,32,1024]{3,2,1,0:T(8,128)(2,1)} %bitcast.167), custom_call_target="tpu_custom_call" | custom-call | tf_op jit(solution)/shard_map/pallas_call | solution.py:678
  269.1 2.1 fusion.14
  272.4 11.3 %shard_map.226 = (f32[8,128]{1,0:T(8,128)}, f32[32,1024]{1,0:T(8,128)}, f32[32,512]{1,0:T(8,128)}, f32[32,512]{1,0:T(8,128)}, f32[32,1024]{1,0:T(8,128)}) custom-call(f32[8,8,128]{2,1,0:T(8,128)} %maximum_maximum_fusion.g, bf16[4,32,512]{2,1,0:T(8,128)(2,1)} %bitcast.189, bf16[32,1024]{1,0:T(8,128)(2,1)} %get-tuple-element.41.w), custom_call_target="tpu_custom_call" | custom-call | tf_op jit(solution)/shard_map/pallas_call | solution.py:779
  292.3 1.9 copy.59
  (192 shorter events, 45.2 us)
Async XLA Ops:
  0.6 119.2 %copy-start = (bf16[576,1024]{1,0:T(8,128)(2,1)S(1)}, bf16[576,1024]{1,0:T(8,128)(2,1)}, u32[]{:S(2)}) copy-start(bf16[576,1024]{1,0:T(8,128)(2,1)} %param.22) | copy-start | bytes 3538948
  30.1 4.5 %copy-start.51 = (bf16[4,2,128,512]{3,2,1,0:T(8,128)(2,1)S(1)}, bf16[4,2,128,512]{3,2,1,0:T(8,128)(2,1)}, u32[]{:S(2)}) copy-start(bf16[4,2,128,512]{3,2,1,0:T(8,128)(2,1)} %get-tuple-element.33) | copy-start | bytes 3145732
  31.5 3.9 %copy-start.27 = (f32[8,1,128]{2,1,0:T(1,128)}, f32[8,1,128]{2,1,0:T(1,128)S(1)}, u32[]{:S(2)}) copy-start(f32[8,1,128]{2,1,0:T(1,128)S(1)} %get-tuple-element.80) | copy-start | bytes 12292
  35.4 4.0 %copy-start.1 = (f32[512,512]{0,1:T(8,128)}, f32[512,512]{0,1:T(8,128)S(1)}, u32[]{:S(2)}) copy-start(f32[512,512]{0,1:T(8,128)S(1)} %fusion.40) | copy-start | bytes 3145732
  35.5 5.9 %copy-start.25 = (bf16[512,2,2,64]{0,3,2,1:T(8,128)(2,1)}, bf16[512,2,2,64]{0,3,2,1:T(8,128)(2,1)S(1)}, u32[]{:S(2)}) copy-start(bf16[512,2,2,64]{0,3,2,1:T(8,128)(2,1)S(1)} %broadcast_in_dim.36) | copy-start | bytes 786436
  36.0 5.5 %copy-start.15 = (pred[512,512]{0,1:T(8,128)(4,1)}, pred[512,512]{0,1:T(8,128)(4,1)S(1)}, u32[]{:S(2)}) copy-start(pred[512,512]{0,1:T(8,128)(4,1)S(1)} %fusion.7) | copy-start | bytes 786436
  44.3 40.4 %copy-start.8 = (bf16[128,1024]{1,0:T(8,128)(2,1)S(1)}, bf16[128,1024]{1,0:T(8,128)(2,1)}, u32[]{:S(2)}) copy-start(bf16[128,1024]{1,0:T(8,128)(2,1)} %refs_3_.1) | copy-start | bytes 786436
  114.9 3.5 %copy-start.48 = (bf16[4,2,128,1024]{3,2,1,0:T(8,128)(2,1)S(1)}, bf16[4,2,128,1024]{3,2,1,0:T(8,128)(2,1)}, u32[]{:S(2)}) copy-start(bf16[4,2,128,1024]{3,2,1,0:T(8,128)(2,1)} %get-tuple-element.36) | copy-start | bytes 6291460
  114.9 3.5 %copy-start.50 = (bf16[576,1024]{1,0:T(8,128)(2,1)S(1)}, bf16[576,1024]{1,0:T(8,128)(2,1)}, u32[]{:S(2)}) copy-start(bf16[576,1024]{1,0:T(8,128)(2,1)} %param.23) | copy-start | bytes 3538948
  208.9 12.4 %copy-start.16 = (pred[512,512]{0,1:T(8,128)(4,1)S(1)}, pred[512,512]{0,1:T(8,128)(4,1)}, u32[]{:S(2)}) copy-start(pred[512,512]{0,1:T(8,128)(4,1)} %copy-done.15) | copy-start | bytes 786436
  208.9 12.4 %copy-start.41 = (f32[4,512]{1,0:T(4,128)S(1)}, f32[4,512]{1,0:T(4,128)}, u32[]{:S(2)}) copy-start(f32[4,512]{1,0:T(4,128)} %copy-done.40) | copy-start | bytes 24580
  221.3 4.2 %copy-start.7 = (f32[4,512,512]{1,2,0:T(8,128)S(1)}, f32[4,512,512]{1,2,0:T(8,128)}, u32[]{:S(2)}) copy-start(f32[4,512,512]{1,2,0:T(8,128)} %copy-done.6) | copy-start | bytes 12582916
  221.3 4.2 %copy-start.26 = (bf16[512,2,2,64]{0,3,2,1:T(8,128)(2,1)S(1)}, bf16[512,2,2,64]{0,3,2,1:T(8,128)(2,1)}, u32[]{:S(2)}) copy-start(bf16[512,2,2,64]{0,3,2,1:T(8,128)(2,1)} %copy-done.25) | copy-start | bytes 786436
  221.3 4.2 %copy-start.42 = (f32[4,512]{1,0:T(4,128)S(1)}, f32[4,512]{1,0:T(4,128)}, u32[]{:S(2)}) copy-start(f32[4,512]{1,0:T(4,128)} %copy-done.40) | copy-start | bytes 24580
  233.1 3.2 %copy-start.3 = (bf16[2,2,128,1024]{3,2,1,0:T(8,128)(2,1)S(1)}, bf16[2,2,128,1024]{3,2,1,0:T(8,128)(2,1)}, u32[]{:S(2)}) copy-start(bf16[2,2,128,1024]{3,2,1,0:T(8,128)(2,1)} %get-tuple-element.31) | copy-start | bytes 3145732
  233.1 3.2 %copy-start.28 = (f32[8,1,128]{2,1,0:T(1,128)S(1)}, f32[8,1,128]{2,1,0:T(1,128)}, u32[]{:S(2)}) copy-start(f32[8,1,128]{2,1,0:T(1,128)} %copy-done.27) | copy-start | bytes 12292
  233.2 3.2 %copy-start.35 = (f32[2,2,128]{2,1,0:T(2,128)S(1)}, f32[2,2,128]{2,1,0:T(2,128)}, u32[]{:S(2)}) copy-start(f32[2,2,128]{2,1,0:T(2,128)} %copy-done.34) | copy-start | bytes 6148
  233.2 3.5 %copy-start.53 = (bf16[512,2,64]{0,2,1:T(8,128)(2,1)S(1)}, bf16[512,2,64]{0,2,1:T(8,128)(2,1)}, u32[]{:S(2)}) copy-start(bf16[512,2,64]{0,2,1:T(8,128)(2,1)} %bitcast_reduce_fusion) | copy-start | bytes 393220
  238.4 29.5 %copy-start.46 = (f32[128]{0:T(128)S(1)}, f32[128]{0:T(128)}, u32[]{:S(2)}) copy-start(f32[128]{0:T(128)} %get-tuple-element.76) | copy-start | bytes 1540
  239.7 29.5 %copy-start.10 = (f32[128,1024]{1,0:T(8,128)S(1)}, f32[128,1024]{1,0:T(8,128)}, u32[]{:S(2)}) copy-start(f32[128,1024]{1,0:T(8,128)} %get-tuple-element.55) | copy-start | bytes 1572868
  239.7 31.6 %copy-start.47 = (f32[128]{0:T(128)S(1)}, f32[128]{0:T(128)}, u32[]{:S(2)}) copy-start(f32[128]{0:T(128)} %get-tuple-element.63) | copy-start | bytes 1540
  239.7 32.1 %copy-start.37 = (f32[1024]{0:T(1024)S(1)}, f32[1024]{0:T(1024)}, u32[]{:S(2)}) copy-start(f32[1024]{0:T(1024)} %get-tuple-element.50) | copy-start | bytes 12292
  269.1 25.1 %copy-start.19 = (f32[144,1024]{1,0:T(8,128)S(1)}, f32[144,1024]{1,0:T(8,128)}, u32[]{:S(2)}) copy-start(f32[144,1024]{1,0:T(8,128)} %get-tuple-element.123) | copy-start | bytes 1769476
  271.3 23.8 %copy-start.18 = (f32[144,1024]{1,0:T(8,128)S(1)}, f32[144,1024]{1,0:T(8,128)}, u32[]{:S(2)}) copy-start(f32[144,1024]{1,0:T(8,128)} %get-tuple-element.124) | copy-start | bytes 1769476
  (30 other events, 45.4 us)
where the time goes:
time: 297 us; the launch traced here: 296 us
  Pallas kernels  206 us (69%)
  matrix products  44.4 us (15%)
  other arithmetic  23.7 us (8%)
  local copies, waits for them, and re-layouts  20.4 us (7%)
    pallas_call x6, Pallas kernels, communicate(): pl.pallas_call(kernel, out_shape=outs, in_specs=[vm] * len(arrays), out_s...  195 us
    unnamed x115, local copies, waits for them, and re-layouts  14.6 us
    dot_general x5, matrix products, dot_nt(): lax.dot_general(left_mat, right_mat, (((1,), (1,)), ((), ())), preferred_...  12.3 us
    pallas_call x1, Pallas kernels, finish(): pl.pallas_call(kernel, out_shape=[jax.ShapeDtypeStruct(gains.shape[1:], F...  11.3 us
    dot_general x5, matrix products, dot_nn(): return jnp.dot(left_mat, right_mat, preferred_element_type=jnp.float32)  10.9 us
    dot_general x5, matrix products, dot_tn(): lax.dot_general(left_mat, right_mat, (((0,), (0,)), ((), ())), preferred_...  10.4 us

commit v1 on v0

--- a/solution.py
+++ b/solution.py
@@ -650,6 +650,17 @@
             pass
 
 
+def grant(items):
+    total = 1 << 20
+    for item in items:
+        if item.dtype in (BF, F32):
+            size = 2 if item.dtype == BF else 4
+            for extent in item.shape:
+                size *= extent
+            total += size
+    return total
+
+
 def communicate(ops, arrays, cid):
     axes = sorted({op.name for op in ops})
     outs = [shape for op in ops for shape in op.outs]
@@ -682,7 +693,9 @@
         out_specs=[vm] * len(outs),
         scratch_shapes=scratch,
         compiler_params=pltpu.CompilerParams(
-            collective_id=cid, has_side_effects=True, vmem_limit_bytes=62 * 1024 * 1024
+            collective_id=cid,
+            has_side_effects=True,
+            vmem_limit_bytes=grant(list(arrays) + outs + scratch),
         ),
     )(*arrays)
 
@@ -795,8 +808,33 @@
             pltpu.VMEM(out_piece.shape, out_piece.dtype),
         ]
         + [dma((F,)), dma((F,)), dma((C,)), dma((C,)), dma((C,)), dma((C,)), dma((1,)), dma((1,))],
-        compiler_params=pltpu.CompilerParams(collective_id=cid, has_side_effects=True),
+        compiler_params=pltpu.CompilerParams(
+            collective_id=cid, has_side_effects=True, vmem_limit_bytes=4 * 1024 * 1024
+        ),
     )(gains, attn_piece, out_piece)
+
+
+def emit(arrays):
+    count = len(arrays)
+
+    def kernel(*refs):
+        sems = refs[2 * count]
+        copies = [
+            pltpu.make_async_copy(refs[i], refs[count + i], sems.at[i]) for i in range(count)
+        ]
+        for copy in copies:
+            copy.start()
+        for copy in copies:
+            copy.wait()
+
+    return pl.pallas_call(
+        kernel,
+        out_shape=[jax.ShapeDtypeStruct(a.shape, a.dtype) for a in arrays],
+        in_specs=[pl.BlockSpec(memory_space=pltpu.VMEM)] * count,
+        out_specs=[pl.BlockSpec(memory_space=pl.ANY)] * count,
+        scratch_shapes=[pltpu.SemaphoreType.DMA((count,))],
+        compiler_params=pltpu.CompilerParams(vmem_limit_bytes=8 * 1024 * 1024),
+    )(*arrays)
 
 
 def on_device(
@@ -977,6 +1015,9 @@
     )
     g_sum, query_grad, key_grad, value_grad, out_proj_grad = finish(
         gains, qkv_sum.reshape(C, rows // C, qw + 2 * kw), wo_sum, qw, kw, 7
+    )
+    query_grad, key_grad, value_grad, out_proj_grad, gate_grad, up_grad, down_grad = emit(
+        [query_grad, key_grad, value_grad, out_proj_grad, gate_grad, up_grad, down_grad]
     )
     return (
         block_output,

time: 297 us -> 254 us (0.86)
  Pallas kernels: 206 us -> 189 us
  matrix products: 44.4 us -> 28.8 us
  local copies, waits for them, and re-layouts: 20.4 us -> 13.5 us
    pallas_call x6, Pallas kernels: 195 us -> 177 us  [communicate(): pl.pallas_call(kernel, out_shape=outs, in_specs=[vm] * len(arrays), out_s...]
    unnamed x115 -> x92, local copies, waits for them, and re-layouts: 14.6 us -> 5.54 us
    dot_general x5, matrix products: 10.4 us -> 5.37 us  [dot_tn(): lax.dot_general(left_mat, right_mat, (((0,), (0,)), ((), ())), preferred_...]
    dot_general x5, matrix products: 12.3 us -> 7.86 us  [dot_nt(): lax.dot_general(left_mat, right_mat, (((1,), (1,)), ((), ())), preferred_...]
    dot_general x5, matrix products: 10.9 us -> 7.08 us  [dot_nn(): return jnp.dot(left_mat, right_mat, preferred_element_type=jnp.float32)]
where the time goes in v1:
time: 254 us; the launch traced here: 253 us
  Pallas kernels  189 us (74%)
  matrix products  28.8 us (11%)
  other arithmetic  20.9 us (8%)
  local copies, waits for them, and re-layouts  13.5 us (5%)
    pallas_call x6, Pallas kernels, communicate(): pl.pallas_call(kernel, out_shape=outs, in_specs=[vm] * len(arrays), out_s...  177 us
    pallas_call x1, Pallas kernels, finish(): pl.pallas_call(kernel, out_shape=[jax.ShapeDtypeStruct(gains.shape[1:], F...  9.86 us
    dot_general x5, matrix products, dot_nt(): lax.dot_general(left_mat, right_mat, (((1,), (1,)), ((), ())), preferred_...  7.86 us
    dot_general x5, matrix products, dot_nn(): return jnp.dot(left_mat, right_mat, preferred_element_type=jnp.float32)  7.08 us
    unnamed x92, local copies, waits for them, and re-layouts  5.54 us
    dot_general x5, matrix products, dot_tn(): lax.dot_general(left_mat, right_mat, (((0,), (0,)), ((), ())), preferred_...  5.37 us

profile of v1, /device:TPU:0, one launch (start us, length us, event | category | flops | bytes accessed | tf_op | source)
XLA Modules:
  0.0 253.5 jit_solution(6578384186389525290)
XLA Ops:
  5.2 22.9 %shard_map.220 = (bf16[4,2,128,512]{3,2,1,0:T(8,128)(2,1)S(1)}, bf16[4,2,16,128]{3,2,1,0:T(8,128)(2,1)S(1)}, bf16[2,128,1024]{2,1,0:T(8,128)(2,1)S(1)}, bf16[2,2,128,1024]{3,2,1,0:T(8,128)(2,1)S(1)}) custom-call(bf16[128,512]{1,0:T(8,128)(2,1)S(1)} %pad_maximum_fusion.10.refs_0_, bf16[16,128]{1,0:T(8,128)(2,1)S(1)} %fusion.26.refs_1_, ...), custom_call_target="tpu_custom_call" | custom-call | tf_op jit(solution)/shard_map/pallas_call | solution.py:689
  43.0 35.5 %shard_map.221 = (f32[128,1024]{1,0:T(8,128)S(1)}, bf16[4,2,128,1024]{3,2,1,0:T(8,128)(2,1)S(1)}) custom-call(bf16[2,2,128,1024]{3,2,1,0:T(8,128)(2,1)S(1)} %bitcast.166, bf16[128,1024]{1,0:T(8,128)(2,1)S(1)} %copy-done.3), custom_call_target="tpu_custom_call" | custom-call | tf_op jit(solution)/shard_map/pallas_call | solution.py:689
  79.3 23.7 %shard_map.222 = bf16[4,2,128,1024]{3,2,1,0:T(8,128)(2,1)S(1)} custom-call(bf16[128,1024]{1,0:T(8,128)(2,1)S(1)} %multiply_convert_fusion.5.refs_0_), custom_call_target="tpu_custom_call" | custom-call | tf_op jit(solution)/shard_map/pallas_call | solution.py:689
  103.1 1.5 fusion.42
  104.6 1.4 fusion.41
  106.0 2.3 multiply_convert_fusion.1
  108.3 1.4 convolution_convert_fusion.3
  109.7 1.4 convolution_convert_fusion.2
  111.1 1.4 convolution_convert_fusion.1
  112.5 1.8 fusion.43
  114.4 1.9 add_convert_fusion
  116.3 2.1 convolution_convert_fusion
  118.4 61.2 %shard_map.223 = (f32[144,1024]{1,0:T(8,128)S(1)}, f32[144,1024]{1,0:T(8,128)S(1)}, f32[144,1024]{1,0:T(8,128)S(1)}, f32[128,1024]{1,0:T(8,128)S(1)}, f32[128,1024]{1,0:T(8,128)S(1)}) custom-call(bf16[2,2,144,1024]{3,2,1,0:T(8,128)(2,1)S(1)} %bitcast.174, bf16[2,2,144,1024]{3,2,1,0:T(8,128)(2,1)S(1)} %bitcast.175, bf16[2,2,144,1024]{3,2,1,0:T(8,128)(2,1)S(1)} %bitcast.176, ...), custom_call_target="tpu_custom_call" | custom-call | tf_op jit(solution)/shard_map/pallas_call | solution.py:689
  181.7 8.5 %shard_map.224 = bf16[2,2,128,1024]{3,2,1,0:T(8,128)(2,1)S(1)} custom-call(bf16[128,1024]{1,0:T(8,128)(2,1)S(1)} %get-tuple-element.68.refs_0_), custom_call_target="tpu_custom_call" | custom-call | tf_op jit(solution)/shard_map/pallas_call | solution.py:689
  190.7 1.8 bitcast_reduce_fusion
  192.6 1.6 multiply_convert_fusion
  195.2 1.7 multiply_reduce_fusion.7
  199.3 2.4 fusion.20
  201.7 2.2 fusion.6
  206.2 1.4 fusion.10
  207.6 2.2 convolution_convert_fusion.6
  211.5 25.7 %shard_map.225 = (f32[128,1024]{1,0:T(8,128)S(1)}, bf16[128,512]{1,0:T(8,128)(2,1)S(1)}, bf16[32,1024]{1,0:T(8,128)(2,1)S(1)}) custom-call(bf16[2,2,128,1024]{3,2,1,0:T(8,128)(2,1)S(1)} %bitcast.177, bf16[4,2,128,512]{3,2,1,0:T(8,128)(2,1)S(1)} %bitcast.178, bf16[4,2,32,1024]{3,2,1,0:T(8,128)(2,1)S(1)} %bitcast.167), custom_call_target="tpu_custom_call" | custom-call | tf_op jit(solution)/shard_map/pallas_call | solution.py:689
  239.0 9.9 %shard_map.226 = (f32[8,128]{1,0:T(8,128)S(1)}, f32[32,1024]{1,0:T(8,128)S(1)}, f32[32,512]{1,0:T(8,128)S(1)}, f32[32,512]{1,0:T(8,128)S(1)}, f32[32,1024]{1,0:T(8,128)S(1)}) custom-call(f32[8,8,128]{2,1,0:T(8,128)S(1)} %maximum_maximum_fusion.g, bf16[4,32,512]{2,1,0:T(8,128)(2,1)S(1)} %bitcast.181, bf16[32,1024]{1,0:T(8,128)(2,1)S(1)} %get-tuple-element.48.w), custom_call_target="tpu_custom_call" | custom-call | tf_op jit(solution)/shard_map/pallas_call | solution.py:792
  251.6 1.4 shard_map.227
  (170 shorter events, 34.7 us)
Async XLA Ops:
  0.6 105.4 %copy-start = (bf16[576,1024]{1,0:T(8,128)(2,1)S(1)}, bf16[576,1024]{1,0:T(8,128)(2,1)}, u32[]{:S(2)}) copy-start(bf16[576,1024]{1,0:T(8,128)(2,1)} %param.22) | copy-start | bytes 3538948
  28.1 14.5 %copy-start.10 = (bf16[2,128,1024]{2,1,0:T(8,128)(2,1)}, bf16[2,128,1024]{2,1,0:T(8,128)(2,1)S(1)}, u32[]{:S(2)}) copy-start(bf16[2,128,1024]{2,1,0:T(8,128)(2,1)S(1)} %get-tuple-element.41) | copy-start | bytes 1572868
  31.7 9.6 %copy-start.26 = (pred[512,512]{0,1:T(8,128)(4,1)}, pred[512,512]{0,1:T(8,128)(4,1)S(1)}, u32[]{:S(2)}) copy-start(pred[512,512]{0,1:T(8,128)(4,1)S(1)} %fusion.7) | copy-start | bytes 786436
  35.5 4.8 %copy-start.18 = (f32[512,32]{0,1:T(8,128)}, f32[512,32]{0,1:T(8,128)S(1)}, u32[]{:S(2)}) copy-start(f32[512,32]{0,1:T(8,128)S(1)} %get-tuple-element.103) | copy-start | bytes 196612
  35.5 4.8 %copy-start.21 = (f32[512,32]{0,1:T(8,128)}, f32[512,32]{0,1:T(8,128)S(1)}, u32[]{:S(2)}) copy-start(f32[512,32]{0,1:T(8,128)S(1)} %get-tuple-element.104) | copy-start | bytes 196612
  35.6 4.7 %copy-start.28 = (bf16[512,2,2,64]{0,3,2,1:T(8,128)(2,1)}, bf16[512,2,2,64]{0,3,2,1:T(8,128)(2,1)S(1)}, u32[]{:S(2)}) copy-start(bf16[512,2,2,64]{0,3,2,1:T(8,128)(2,1)S(1)} %broadcast_in_dim.39) | copy-start | bytes 786436
  36.4 3.9 %copy-start.36 = (f32[64]{0:T(128)}, f32[64]{0:T(128)S(1)}, u32[]{:S(2)}) copy-start(f32[64]{0:T(128)S(1)} %slice.69) | copy-start | bytes 772
  42.5 147.7 %copy-start.24 = (bf16[4,64,512]{2,1,0:T(8,128)(2,1)}, bf16[4,64,512]{2,1,0:T(8,128)(2,1)S(1)}, u32[]{:S(2)}) copy-start(bf16[4,64,512]{2,1,0:T(8,128)(2,1)S(1)} %convolution_convert_fusion.10) | copy-start | bytes 786436
  42.5 36.0 %copy-start.2 = (bf16[128,1024]{1,0:T(8,128)(2,1)S(1)}, bf16[128,1024]{1,0:T(8,128)(2,1)}, u32[]{:S(2)}) copy-start(bf16[128,1024]{1,0:T(8,128)(2,1)} %refs_3_.1) | copy-start | bytes 786436
  78.5 24.6 %copy-start.42 = (bf16[576,1024]{1,0:T(8,128)(2,1)S(1)}, bf16[576,1024]{1,0:T(8,128)(2,1)}, u32[]{:S(2)}) copy-start(bf16[576,1024]{1,0:T(8,128)(2,1)} %param.21) | copy-start | bytes 3538948
  179.6 10.5 %copy-start.4 = (f32[144,1024]{1,0:T(8,128)}, f32[144,1024]{1,0:T(8,128)S(1)}, u32[]{:S(2)}) copy-start(f32[144,1024]{1,0:T(8,128)S(1)} %get-tuple-element.54.refs_4_) | copy-start | bytes 1769476
  179.6 10.5 %copy-start.6 = (f32[144,1024]{1,0:T(8,128)}, f32[144,1024]{1,0:T(8,128)S(1)}, u32[]{:S(2)}) copy-start(f32[144,1024]{1,0:T(8,128)S(1)} %get-tuple-element.55.refs_5_) | copy-start | bytes 1769476
  179.7 10.5 %copy-start.8 = (f32[144,1024]{1,0:T(8,128)}, f32[144,1024]{1,0:T(8,128)S(1)}, u32[]{:S(2)}) copy-start(f32[144,1024]{1,0:T(8,128)S(1)} %get-tuple-element.56.refs_6_) | copy-start | bytes 1769476
  180.5 9.7 %copy-start.11 = (bf16[2,128,1024]{2,1,0:T(8,128)(2,1)S(1)}, bf16[2,128,1024]{2,1,0:T(8,128)(2,1)}, u32[]{:S(2)}) copy-start(bf16[2,128,1024]{2,1,0:T(8,128)(2,1)} %copy-done.10) | copy-start | bytes 1572868
  181.7 9.0 %copy-start.27 = (pred[512,512]{0,1:T(8,128)(4,1)S(1)}, pred[512,512]{0,1:T(8,128)(4,1)}, u32[]{:S(2)}) copy-start(pred[512,512]{0,1:T(8,128)(4,1)} %copy-done.26) | copy-start | bytes 786436
  194.1 2.8 %copy-start.16 = (bf16[4,512,512]{1,2,0:T(8,128)(2,1)}, bf16[4,512,512]{1,2,0:T(8,128)(2,1)S(1)}, u32[]{:S(2)}) copy-start(bf16[4,512,512]{1,2,0:T(8,128)(2,1)S(1)} %multiply_convert_fusion) | copy-start | bytes 6291460
  194.2 5.2 %copy-start.32 = (f32[512,2]{0,1:T(2,128)S(1)}, f32[512,2]{0,1:T(2,128)}, u32[]{:S(2)}) copy-start(f32[512,2]{0,1:T(2,128)} %copy-done.31) | copy-start | bytes 12292
  199.3 4.6 %copy-start.20 = (f32[512,32]{0,1:T(8,128)S(1)}, f32[512,32]{0,1:T(8,128)}, u32[]{:S(2)}) copy-start(f32[512,32]{0,1:T(8,128)} %copy-done.18) | copy-start | bytes 196612
  199.3 4.6 %copy-start.23 = (f32[512,32]{0,1:T(8,128)S(1)}, f32[512,32]{0,1:T(8,128)}, u32[]{:S(2)}) copy-start(f32[512,32]{0,1:T(8,128)} %copy-done.21) | copy-start | bytes 196612
  211.0 26.2 %copy-start.40 = (f32[128]{0:T(128)S(1)}, f32[128]{0:T(128)}, u32[]{:S(2)}) copy-start(f32[128]{0:T(128)} %get-tuple-element.90) | copy-start | bytes 1540
  211.5 26.0 %copy-start.17 = (f32[128,1024]{1,0:T(8,128)S(1)}, f32[128,1024]{1,0:T(8,128)}, u32[]{:S(2)}) copy-start(f32[128,1024]{1,0:T(8,128)} %get-tuple-element.69) | copy-start | bytes 1572868
  211.5 27.0 %copy-start.41 = (f32[128]{0:T(128)S(1)}, f32[128]{0:T(128)}, u32[]{:S(2)}) copy-start(f32[128]{0:T(128)} %get-tuple-element.77) | copy-start | bytes 1540
  211.5 27.4 %copy-start.35 = (f32[1024]{0:T(1024)S(1)}, f32[1024]{0:T(1024)}, u32[]{:S(2)}) copy-start(f32[1024]{0:T(1024)} %get-tuple-element.64) | copy-start | bytes 12292
  237.2 12.2 %copy-start.5 = (f32[144,1024]{1,0:T(8,128)S(1)}, f32[144,1024]{1,0:T(8,128)}, u32[]{:S(2)}) copy-start(f32[144,1024]{1,0:T(8,128)} %copy-done.4) | copy-start | bytes 1769476
  (22 other events, 35.2 us)

commit v2 on v1

--- a/solution.py
+++ b/solution.py
@@ -927,9 +927,9 @@
     o_local = jnp.einsum("hqk,khd->qhd", prob_bf, v_local, preferred_element_type=F32).astype(BF)
     o_flat = o_local.reshape(G, qw)
     part = dot_nn(o_flat, wo).astype(BF).reshape(CL, CD, T, W)
-    attn_sum, dy_all = communicate(
-        [Reduce("ctx", (T, W), BF, 2), Gather("fsdp", (T, W), BF, "both")],
-        [part, out_cotangent],
+    dy_all, attn_sum = communicate(
+        [Gather("fsdp", (T, W), BF, "both"), Reduce("ctx", (T, W), BF, 2)],
+        [out_cotangent, part],
         2,
     )
     dy_all = dy_all.reshape(F * T, W)
@@ -958,15 +958,13 @@
     back_part = (
         (dot_nn(d_gate, gate_proj) + dot_nn(d_up, up_proj)).astype(BF).reshape(L, D, T, W)
     )
-    gate_grad, up_grad, down_grad, d_ffn_in, ffn_out = communicate(
+    gate_grad, d_ffn_in, ffn_out = communicate(
         [
             Reduce("ctx", (ffc, W), BF),
-            Reduce("ctx", (ffc, W), BF),
-            Reduce("ctx", (ffc, W), BF),
-            Reduce("fsdp", (T, W), BF, 4),
-            Reduce("fsdp", (T, W), BF, 4, 0, 4),
+            Reduce("fsdp", (T, W), BF, 4, 1),
+            Reduce("fsdp", (T, W), BF, 4, 1),
         ],
-        grads + [back_part, down_part],
+        grads[:1] + [back_part, down_part],
         4,
     )
     block_output = (mixed_res + ffn_out).astype(BF)
@@ -993,13 +991,15 @@
     dn_part = dot_nt(d_qkv, w_all).astype(BF).reshape(CL, CD, T, W)
     qkv_part = dot_tn(normed, d_qkv).astype(BF).reshape(L, D, rows, qw + 2 * kw)
     wo_part = dot_tn(o_flat, dm_all).astype(BF).reshape(L, D, qw // F, W)
-    d_normed, qkv_sum, wo_sum = communicate(
+    d_normed, qkv_sum, wo_sum, up_grad, down_grad = communicate(
         [
             Reduce("ctx", (T, W), BF),
-            Reduce("fsdp", qkv_part.shape[2:], BF, 2, 0, 0, BF),
-            Reduce("fsdp", wo_part.shape[2:], BF, 1, 1, 0, BF),
+            Reduce("fsdp", qkv_part.shape[2:], BF, 2, 1, 0, BF),
+            Reduce("fsdp", wo_part.shape[2:], BF, 1, 0, 0, BF),
+            Reduce("ctx", (ffc, W), BF),
+            Reduce("ctx", (ffc, W), BF),
         ],
-        [dn_part, qkv_part, wo_part],
+        [dn_part, qkv_part, wo_part] + grads[1:],
         6,
     )
     grad_gain_attn = jnp.sum(d_normed * x_float * inv_one, axis=0)

time: 254 us -> 239 us (0.941)
  other arithmetic: 20.9 us -> 13.8 us
  local copies, waits for them, and re-layouts: 13.5 us -> 9.99 us
  Pallas kernels: 189 us -> 186 us
    pallas_call x6, Pallas kernels: 177 us -> 175 us  [communicate(): pl.pallas_call(kernel, out_shape=outs, in_specs=[vm] * len(arrays), out_s...]
    unnamed x92 -> x48, local copies, waits for them, and re-layouts: 5.54 us -> 5.41 us
where the time goes in v2:
time: 239 us; the launch traced here: 238 us
  Pallas kernels  186 us (78%)
  matrix products  27.4 us (11%)
  other arithmetic  13.8 us (6%)
  local copies, waits for them, and re-layouts  9.99 us (4%)
    pallas_call x6, Pallas kernels, communicate(): pl.pallas_call(kernel, out_shape=outs, in_specs=[vm] * len(arrays), out_s...  175 us
    pallas_call x1, Pallas kernels, finish(): pl.pallas_call(kernel, out_shape=[jax.ShapeDtypeStruct(gains.shape[1:], F...  9.41 us
    dot_general x5, matrix products, dot_tn(): lax.dot_general(left_mat, right_mat, (((0,), (0,)), ((), ())), preferred_...  7.47 us
    dot_general x5, matrix products, dot_nn(): return jnp.dot(left_mat, right_mat, preferred_element_type=jnp.float32)  7.15 us
    dot_general x5, matrix products, dot_nt(): lax.dot_general(left_mat, right_mat, (((1,), (1,)), ((), ())), preferred_...  6.48 us
    unnamed x48, local copies, waits for them, and re-layouts  5.41 us

profile of v2, /device:TPU:0, one launch (start us, length us, event | category | flops | bytes accessed | tf_op | source)
XLA Modules:
  0.0 238.1 jit_solution(14899667063566124774)
XLA Ops:
  7.9 22.9 %shard_map.220 = (bf16[4,2,128,512]{3,2,1,0:T(8,128)(2,1)S(1)}, bf16[4,2,16,128]{3,2,1,0:T(8,128)(2,1)S(1)}, bf16[2,128,1024]{2,1,0:T(8,128)(2,1)S(1)}, bf16[2,2,128,1024]{3,2,1,0:T(8,128)(2,1)S(1)}) custom-call(bf16[128,512]{1,0:T(8,128)(2,1)S(1)} %pad_maximum_fusion.10.refs_0_, bf16[16,128]{1,0:T(8,128)(2,1)S(1)} %fusion.26.refs_1_, ...), custom_call_target="tpu_custom_call" | custom-call | tf_op jit(solution)/shard_map/pallas_call | solution.py:689
  33.0 1.3 fusion.4
  37.8 1.3 convolution_convert_fusion.10
  39.6 35.5 %shard_map.221 = (bf16[4,2,128,1024]{3,2,1,0:T(8,128)(2,1)S(1)}, f32[128,1024]{1,0:T(8,128)S(1)}) custom-call(bf16[128,1024]{1,0:T(8,128)(2,1)S(1)} %copy-done.5, bf16[2,2,128,1024]{3,2,1,0:T(8,128)(2,1)S(1)} %bitcast.166), custom_call_target="tpu_custom_call" | custom-call | tf_op jit(solution)/shard_map/pallas_call | solution.py:689
  76.0 23.7 %shard_map.222 = bf16[4,2,128,1024]{3,2,1,0:T(8,128)(2,1)S(1)} custom-call(bf16[128,1024]{1,0:T(8,128)(2,1)S(1)} %multiply_convert_fusion.5.refs_0_), custom_call_target="tpu_custom_call" | custom-call | tf_op jit(solution)/shard_map/pallas_call | solution.py:689
  99.7 1.4 fusion.42
  101.2 1.4 fusion.41
  102.6 2.3 multiply_convert_fusion.1
  104.9 2.4 %convolution_convert_fusion.1 = bf16[576,1024]{1,0:T(8,128)(2,1)} fusion(bf16[1024,576]{0,1:T(8,128)(2,1)S(1)} %get-tuple-element.72, bf16[1024,1024]{1,0:T(8,128)(2,1)S(1)} %bitcast.185), kind=kOutput, calls=%fused_computation.18 | convolution fusion | flops 1208549376 | bytes 4456448 | tf_op jit(solution)/shard_map/dot_general | solution.py:80
  107.4 1.8 convolution_convert_fusion
  109.2 1.4 convolution_convert_fusion.3
  110.6 2.4 %convolution_convert_fusion.2 = bf16[576,1024]{1,0:T(8,128)(2,1)} fusion(bf16[1024,576]{0,1:T(8,128)(2,1)S(1)} %get-tuple-element.74, bf16[1024,1024]{1,0:T(8,128)(2,1)S(1)} %bitcast.171), kind=kOutput, calls=%fused_computation.19 | convolution fusion | flops 1208549376 | bytes 4456448 | tf_op jit(solution)/shard_map/dot_general | solution.py:80
  113.1 1.8 fusion.43
  114.9 2.3 add_convert_fusion
  117.2 53.7 %shard_map.223 = (f32[144,1024]{1,0:T(8,128)S(1)}, f32[128,1024]{1,0:T(8,128)S(1)}, f32[128,1024]{1,0:T(8,128)S(1)}) custom-call(bf16[2,2,144,1024]{3,2,1,0:T(8,128)(2,1)S(1)} %bitcast.176, bf16[4,2,128,1024]{3,2,1,0:T(8,128)(2,1)S(1)} %bitcast.173, bf16[4,2,128,1024]{3,2,1,0:T(8,128)(2,1)S(1)} %bitcast.172), custom_call_target="tpu_custom_call" | custom-call | tf_op jit(solution)/shard_map/pallas_call | solution.py:689
  171.0 1.2 fusion.38
  172.2 7.8 %shard_map.224 = bf16[2,2,128,1024]{3,2,1,0:T(8,128)(2,1)S(1)} custom-call(bf16[128,1024]{1,0:T(8,128)(2,1)S(1)} %get-tuple-element.68.refs_0_), custom_call_target="tpu_custom_call" | custom-call | tf_op jit(solution)/shard_map/pallas_call | solution.py:689
  181.0 1.2 bitcast_reduce_fusion
  182.2 1.6 multiply_convert_fusion
  187.0 1.2 fusion.20
  190.6 31.4 %shard_map.225 = (f32[128,1024]{1,0:T(8,128)S(1)}, bf16[128,512]{1,0:T(8,128)(2,1)S(1)}, bf16[32,1024]{1,0:T(8,128)(2,1)S(1)}, f32[144,1024]{1,0:T(8,128)S(1)}, f32[144,1024]{1,0:T(8,128)S(1)}) custom-call(bf16[2,2,128,1024]{3,2,1,0:T(8,128)(2,1)S(1)} %bitcast.178, bf16[4,2,128,512]{3,2,1,0:T(8,128)(2,1)S(1)} %bitcast.177, ...), custom_call_target="tpu_custom_call" | custom-call | tf_op jit(solution)/shard_map/pallas_call | solution.py:689
  224.0 2.2 fusion.14
  226.3 9.4 %shard_map.226 = (f32[8,128]{1,0:T(8,128)S(1)}, f32[32,1024]{1,0:T(8,128)S(1)}, f32[32,512]{1,0:T(8,128)S(1)}, f32[32,512]{1,0:T(8,128)S(1)}, f32[32,1024]{1,0:T(8,128)S(1)}) custom-call(f32[8,8,128]{2,1,0:T(8,128)S(1)} %maximum_maximum_fusion.g, bf16[4,32,512]{2,1,0:T(8,128)(2,1)S(1)} %bitcast.181, bf16[32,1024]{1,0:T(8,128)(2,1)S(1)} %get-tuple-element.48.w), custom_call_target="tpu_custom_call" | custom-call | tf_op jit(solution)/shard_map/pallas_call | solution.py:792
  235.7 1.4 shard_map.227
  (126 shorter events, 23.9 us)
Async XLA Ops:
  0.6 102.0 %copy-start = (bf16[576,1024]{1,0:T(8,128)(2,1)S(1)}, bf16[576,1024]{1,0:T(8,128)(2,1)}, u32[]{:S(2)}) copy-start(bf16[576,1024]{1,0:T(8,128)(2,1)} %param.22) | copy-start | bytes 3538948
  6.0 1.0 copy-start.1
  7.0 0.9 copy-start.12
  30.8 1.0 copy-start.13
  31.8 7.3 %copy-start.10 = (bf16[2,128,1024]{2,1,0:T(8,128)(2,1)}, bf16[2,128,1024]{2,1,0:T(8,128)(2,1)S(1)}, u32[]{:S(2)}) copy-start(bf16[2,128,1024]{2,1,0:T(8,128)(2,1)S(1)} %get-tuple-element.41) | copy-start | bytes 1572868
  33.0 1.6 copy-start.14
  35.4 150.0 %copy-start.16 = (f32[512,512]{0,1:T(8,128)}, f32[512,512]{0,1:T(8,128)S(1)}, u32[]{:S(2)}) copy-start(f32[512,512]{0,1:T(8,128)S(1)} %fusion.40) | copy-start | bytes 3145732
  37.8 1.8 copy-start.5
  39.1 36.0 %copy-start.2 = (bf16[128,1024]{1,0:T(8,128)(2,1)S(1)}, bf16[128,1024]{1,0:T(8,128)(2,1)}, u32[]{:S(2)}) copy-start(bf16[128,1024]{1,0:T(8,128)(2,1)} %refs_3_.1) | copy-start | bytes 786436
  75.1 24.6 %copy-start.23 = (bf16[576,1024]{1,0:T(8,128)(2,1)S(1)}, bf16[576,1024]{1,0:T(8,128)(2,1)}, u32[]{:S(2)}) copy-start(bf16[576,1024]{1,0:T(8,128)(2,1)} %param.21) | copy-start | bytes 3538948
  99.7 1.4 copy-start.22
  171.0 9.0 %copy-start.11 = (bf16[2,128,1024]{2,1,0:T(8,128)(2,1)S(1)}, bf16[2,128,1024]{2,1,0:T(8,128)(2,1)}, u32[]{:S(2)}) copy-start(bf16[2,128,1024]{2,1,0:T(8,128)(2,1)} %copy-done.10) | copy-start | bytes 1572868
  185.2 1.8 copy-start.20
  185.8 2.4 %copy-start.17 = (bf16[512,1024]{1,0:T(8,128)(2,1)S(1)}, bf16[512,1024]{1,0:T(8,128)(2,1)}, u32[]{:S(2)}) copy-start(bf16[512,1024]{1,0:T(8,128)(2,1)} %fusion.4) | copy-start | bytes 3145732
  187.0 2.0 copy-start.15
  189.0 1.3 copy-start.3
  189.0 1.6 copy-start.4
  190.6 33.2 %copy-start.18 = (f32[128]{0:T(128)S(1)}, f32[128]{0:T(128)}, u32[]{:S(2)}) copy-start(f32[128]{0:T(128)} %get-tuple-element.106) | copy-start | bytes 1540
  190.6 33.4 %copy-start.21 = (f32[128]{0:T(128)S(1)}, f32[128]{0:T(128)}, u32[]{:S(2)}) copy-start(f32[128]{0:T(128)} %get-tuple-element.105) | copy-start | bytes 1540
  222.0 0.8 copy-start.6
  222.8 0.8 copy-start.8
  223.6 2.6 %copy-start.19 = (f32[8]{0:T(128)S(1)}, f32[8]{0:T(128)}, u32[]{:S(2)}) copy-start(f32[8]{0:T(128)} %pad.13.clone) | copy-start | bytes 100
  223.8 11.9 %copy-start.7 = (f32[144,1024]{1,0:T(8,128)S(1)}, f32[144,1024]{1,0:T(8,128)}, u32[]{:S(2)}) copy-start(f32[144,1024]{1,0:T(8,128)} %copy-done.6) | copy-start | bytes 1769476
  223.8 11.9 %copy-start.9 = (f32[144,1024]{1,0:T(8,128)S(1)}, f32[144,1024]{1,0:T(8,128)}, u32[]{:S(2)}) copy-start(f32[144,1024]{1,0:T(8,128)} %copy-done.8) | copy-start | bytes 1769476
